TPU v7x, 256 devices: a whole 4x4x8 slice. The times are simulated.
256 devices in a mesh: dp: 64 (over z, y, x_hi), strip: 4 (over x_lo, core).
Axes of the slice: x: 4 (x_hi: 2, x_lo: 2; x = x_hi * 2 + x_lo), y: 4, z: 8, core: 2. Of those that a mesh axis runs over, the one named last changes fastest.
Arguments:
- images: bfloat16 [256, 3, 32, 128], P('dp', None, 'strip'), may hold values from -16 to 16
- perturbation: float32 [3, 32, 128], P(None, 'strip'), may hold values from -0.5 to 0.5
- labels: int32 [256], P(('dp', 'strip')), may hold values from 0 to 61
- step_levels: int32 [3], replicated, may hold values from 1 to 4
- stem_weight: bfloat16 [48, 192], replicated, may hold values from -0.875 to 0.875
- stem_gain: float32 [192], replicated, may hold values from 0.25 to 1.75
- dw1_kernel: bfloat16 [49, 192], replicated, may hold values from -0.875 to 0.875
- norm1_gain: float32 [192], replicated, may hold values from 0.25 to 1.75
- up1_weight: bfloat16 [192, 768], replicated, may hold values from -0.4375 to 0.4375
- down1_weight: bfloat16 [768, 192], replicated, may hold values from -0.21875 to 0.21875
- scale1: float32 [192], replicated, may hold values from 0.3 to 1
- down_gain: float32 [192], replicated, may hold values from 0.25 to 1.75
- ds_weight: bfloat16 [768, 384], replicated, may hold values from -0.21875 to 0.21875
- head_gain: float32 [384], replicated, may hold values from 0.25 to 1.75
- head_weight: bfloat16 [384, 62], replicated, may hold values from -0.3125 to 0.3125
Outputs:
- new_perturbation: float32 [3, 32, 128], P(None, 'strip')
- losses: float32 [256], P(('dp', 'strip'))
- stem_grad: float32 [48, 192], P(None, 'dp')
- dw1_grad: float32 [49, 192], P(None, 'dp')
- up1_grad: float32 [192, 768], P(None, 'dp')
- down1_grad: float32 [768, 192], P('dp')
- ds_grad: float32 [768, 384], P(None, 'dp')
- head_grad: float32 [384, 62], P('dp')
All inputs are finite; a program needn't handle non-finite values.
Results may differ from a plain program's by a relative error of at most 0.013.
Values may be sent and summed in bfloat16 or wider, within the bound.
A program may use at most 64 MiB of HBM per device.

v0:
```python
import jax
import jax.numpy as jnp
from jax import lax
from jax.sharding import PartitionSpec as P

KS = 7
PATCH = 4
EPS_NORM = 1e-06
EPS_ROOT = 1e-12
BOUND = 0.5
STEP_UNIT = 0.1


def norm_gain(values_in, gain_vec):
    centre = jnp.mean(values_in, axis=-1, keepdims=True)
    centred = values_in - centre
    spread = jnp.mean(centred * centred, axis=-1, keepdims=True)
    return centred * lax.rsqrt(spread + EPS_NORM) * gain_vec


def norm_back(values_in, gain_vec, grad_out):

    def apply_norm(argument):
        return norm_gain(argument, gain_vec)

    return jax.vjp(apply_norm, values_in)[1](grad_out)[0]


def dense(values_in, weight):
    flattened = values_in.astype(jnp.bfloat16).reshape(-1, values_in.shape[-1])
    result = jnp.dot(flattened, weight, preferred_element_type=jnp.float32)
    return result.reshape(values_in.shape[:-1] + (weight.shape[1],))


def dense_back(grad_out, values_in, weight):
    grads_low = grad_out.astype(jnp.bfloat16).reshape(-1, grad_out.shape[-1])
    inputs_low = values_in.astype(jnp.bfloat16).reshape(-1, values_in.shape[-1])
    grad_in = jnp.dot(grads_low, weight.T, preferred_element_type=jnp.float32)
    grad_weight = jnp.dot(inputs_low.T, grads_low, preferred_element_type=jnp.float32)
    return (grad_in.reshape(values_in.shape), grad_weight)


def gelu_exact(values_in):
    return jax.nn.gelu(values_in, approximate=False)


def gelu_back(values_in, grad_out):
    return jax.vjp(gelu_exact, values_in)[1](grad_out)[0]


def depthwise(padded, kernel):
    channels = kernel.shape[1]
    taps = kernel.reshape(KS, KS, 1, channels)
    return lax.conv_general_dilated(
        padded,
        taps,
        (1, 1),
        "VALID",
        dimension_numbers=("NHWC", "HWIO", "NHWC"),
        feature_group_count=channels,
        precision=lax.Precision.HIGHEST,
    )


def flipped(kernel):
    channels = kernel.shape[1]
    return kernel.reshape(KS, KS, channels)[::-1, ::-1].reshape(KS * KS, channels)


def kernel_back(padded, kernel, grad_out):

    def apply_taps(argument):
        return depthwise(padded, argument)

    return jax.vjp(apply_taps, kernel)[1](grad_out)[0]


def pad_both(values_in):
    half = KS // 2
    return jnp.pad(values_in, ((0, 0), (half, half), (half, half), (0, 0)))


def patchify(pixels):
    number, channels, row_count, col_count = pixels.shape
    blocks = pixels.reshape(number, channels, row_count // PATCH, PATCH, col_count // PATCH, PATCH)
    return blocks.transpose(0, 2, 4, 1, 3, 5).reshape(
        number, row_count // PATCH, col_count // PATCH, channels * PATCH * PATCH
    )


def unpatchify(grads_in, channels):
    number, row_count, col_count, _ = grads_in.shape
    blocks = grads_in.reshape(number, row_count, col_count, channels, PATCH, PATCH)
    return blocks.transpose(0, 3, 1, 4, 2, 5).reshape(
        number, channels, row_count * PATCH, col_count * PATCH
    )


def merge_pairs(values_in):
    number, row_count, col_count, channels = values_in.shape
    blocks = values_in.reshape(number, row_count // 2, 2, col_count // 2, 2, channels)
    return blocks.transpose(0, 1, 3, 2, 4, 5).reshape(
        number, row_count // 2, col_count // 2, 4 * channels
    )


def split_pairs(grads_in, channels):
    number, row_count, col_count, _ = grads_in.shape
    blocks = grads_in.reshape(number, row_count, col_count, 2, 2, channels)
    return blocks.transpose(0, 1, 3, 2, 4, 5).reshape(
        number, row_count * 2, col_count * 2, channels
    )


def block_forward(inputs, padded, kernel, gain_vec, w_up, w_down, layer_scale):
    mixed_out = depthwise(padded, kernel)
    normed = norm_gain(mixed_out, gain_vec)
    upper_in = dense(normed, w_up)
    hidden = gelu_exact(upper_in)
    branch = dense(hidden, w_down)
    return (inputs + layer_scale * branch, (mixed_out, normed, upper_in, hidden))


def block_backward(grad_out, padded, kernel, gain_vec, w_up, w_down, layer_scale, stored):
    mixed_out, normed, upper_in, hidden = stored
    grad_branch = grad_out * layer_scale
    grad_hidden, grad_down = dense_back(grad_branch, hidden, w_down)
    grad_upper = gelu_back(upper_in, grad_hidden)
    grad_normed, grad_up = dense_back(grad_upper, normed, w_up)
    grad_mixed = norm_back(mixed_out, gain_vec, grad_normed)
    grad_kernel = kernel_back(padded, kernel, grad_mixed)
    return (grad_mixed, grad_kernel, grad_up, grad_down)


def section_two(held, labels, down_gain, ds_weight, head_gain, head_weight):
    source = held.astype(jnp.float32)
    normed_in = norm_gain(source, down_gain)
    merged = merge_pairs(normed_in)
    start_two = dense(merged, ds_weight)
    pooled = jnp.mean(start_two, axis=(1, 2))
    head_in = norm_gain(pooled, head_gain)
    logits = dense(head_in, head_weight)
    onehot = (labels[:, None] == lax.iota(jnp.int32, logits.shape[1])[None, :]).astype(jnp.float32)
    losses = jax.nn.logsumexp(logits, axis=1) - jnp.sum(onehot * logits, axis=1)
    grad_logits = jax.nn.softmax(logits, axis=1) - onehot
    grad_head_in, grad_head = dense_back(grad_logits, head_in, head_weight)
    grad_pooled = norm_back(pooled, head_gain, grad_head_in)
    cells = start_two.shape[1] * start_two.shape[2]
    grad_start = jnp.broadcast_to((grad_pooled / cells)[:, None, None, :], start_two.shape)
    grad_merged, grad_ds = dense_back(grad_start, merged, ds_weight)
    grad_normed_in = split_pairs(grad_merged, source.shape[3])
    grad_source = norm_back(source, down_gain, grad_normed_in)
    grad_held = lax.optimization_barrier(grad_source.astype(jnp.bfloat16))
    return (losses, grad_held, (grad_ds, grad_head))


def on_device(
    images,
    perturbation,
    labels,
    step_levels,
    stem_weight,
    stem_gain,
    dw1_kernel,
    norm1_gain,
    up1_weight,
    down1_weight,
    scale1,
    down_gain,
    ds_weight,
    head_gain,
    head_weight,
):
    kernel_one = dw1_kernel.astype(jnp.float32)
    pixels = lax.all_to_all(images, "strip", split_axis=0, concat_axis=2, tiled=True)
    whole_delta = lax.all_gather(perturbation, "strip", axis=1, tiled=True)
    perturbed = pixels.astype(jnp.float32) + whole_delta[None]
    patches = patchify(perturbed)
    stem_pre = dense(patches, stem_weight)
    stem_out = lax.optimization_barrier(norm_gain(stem_pre, stem_gain).astype(jnp.bfloat16))
    padded_one = pad_both(stem_out).astype(jnp.float32)
    block_out, stored_one = block_forward(
        stem_out.astype(jnp.float32),
        padded_one,
        kernel_one,
        norm1_gain,
        up1_weight,
        down1_weight,
        scale1,
    )
    section_out = lax.optimization_barrier(block_out.astype(jnp.bfloat16))
    losses, grad_held, grads_two = section_two(
        section_out, labels, down_gain, ds_weight, head_gain, head_weight
    )
    grad_block = grad_held.astype(jnp.float32)
    grad_mixed, grad_dw1, grad_up1, grad_down1 = block_backward(
        grad_block, padded_one, kernel_one, norm1_gain, up1_weight, down1_weight, scale1, stored_one
    )
    grad_stem = grad_block + depthwise(pad_both(grad_mixed), flipped(kernel_one))
    grad_pre = norm_back(stem_pre, stem_gain, grad_stem)
    grad_patches, grad_stem_weight = dense_back(grad_pre, patches, stem_weight)
    grad_pixels = unpatchify(grad_patches, 3)
    delta_part = lax.psum_scatter(
        jnp.sum(grad_pixels, axis=0).astype(jnp.bfloat16), "strip", scatter_dimension=1, tiled=True
    ).astype(jnp.float32)
    grad_ds, grad_head = grads_two
    shares = (
        lax.psum_scatter(grad_stem_weight, "dp", scatter_dimension=1, tiled=True),
        lax.psum_scatter(grad_dw1, "dp", scatter_dimension=1, tiled=True),
        lax.psum_scatter(grad_up1, "dp", scatter_dimension=1, tiled=True),
        lax.psum_scatter(grad_down1, "dp", scatter_dimension=0, tiled=True),
        lax.psum_scatter(grad_ds, "dp", scatter_dimension=1, tiled=True),
        lax.psum_scatter(grad_head, "dp", scatter_dimension=0, tiled=True),
    )
    summed = (
        lax.psum(shares[0].astype(jnp.bfloat16), "strip").astype(jnp.float32),
        lax.psum(shares[1].astype(jnp.bfloat16), "strip").astype(jnp.float32),
        lax.psum(shares[2].astype(jnp.bfloat16), "strip").astype(jnp.float32),
        lax.psum(shares[3].astype(jnp.bfloat16), "strip").astype(jnp.float32),
        lax.psum(shares[4].astype(jnp.bfloat16), "strip").astype(jnp.float32),
        lax.psum(shares[5].astype(jnp.bfloat16), "strip").astype(jnp.float32),
    )
    stem_grad, dw1_grad, up1_grad, down1_grad, ds_grad, head_grad = summed
    levels = STEP_UNIT * step_levels.astype(jnp.float32)
    summed_delta = lax.psum(delta_part, "dp")
    squares = lax.psum(jnp.sum(summed_delta * summed_delta), "strip")
    cells = delta_part.size * lax.axis_size("strip")
    spread = jnp.sqrt(squares / cells + EPS_ROOT)
    new_perturbation = jnp.clip(
        perturbation + levels[:, None, None] * summed_delta / spread, -BOUND, BOUND
    )
    return (new_perturbation, losses, stem_grad, dw1_grad, up1_grad, down1_grad, ds_grad, head_grad)


def solution(mesh):
    return jax.shard_map(
        on_device,
        mesh=mesh,
        in_specs=(
            P("dp", None, "strip", None),
            P(None, "strip", None),
            P(("dp", "strip")),
            P(),
            P(),
            P(),
            P(),
            P(),
            P(),
            P(),
            P(),
            P(),
            P(),
            P(),
            P(),
        ),
        out_specs=(
            P(None, "strip", None),
            P(("dp", "strip")),
            P(None, "dp"),
            P(None, "dp"),
            P(None, "dp"),
            P("dp", None),
            P(None, "dp"),
            P("dp", None),
        ),
        check_vma=False,
    )
```

profile of v0, /device:TPU:9, one launch (start us, length us, event | category | flops | bytes accessed | tf_op | source)
XLA Modules:
  0.0 821.1 jit_solution(3639042860239779611)
XLA Ops:
  0.6 4.0 all-to-all-start
  15.5 5.4 all_gather.3
  20.9 1.7 convert_element_type.200
  24.2 4.8 fusion.63
  30.6 2.9 multiply_convert_fusion
  41.4 1.8 fusion.53
  51.3 179.0 %fusion.51 = (f32[192,16]{0,1:T(8,128)S(1)}, f32[16,192]{1,0:T(8,128)S(1)}, f32[768,8]{0,1:T(8,128)S(1)}) fusion(f32[192,768]{0,1:T(8,128)S(1)} %convolution_bitcast_fusion.2, f32[768,192]{1,0:T(8,128)} %convolution_bitcast_fusion.1, f32[768,384]{0,1:T(8,128)S(1)} %convolution_bitcast_fusion), kind=kCustom, calls=%all-reduce-scatter.3 | all-reduce-scatter fusion | flops 786434 | bytes 2409472
  231.8 4.2 collective-permute-start.13
  236.0 1.7 collective-permute-start.12
  240.3 9.7 %convolution_reduce_fusion = f32[7,7,192]{2,1,0:T(8,128)S(1)} fusion(bf16[1,8,32,192]{3,2,1,0:T(8,128)(2,1)S(1)} %copy-done.6, f32[1,8,32,192]{3,0,2,1:T(1,128)S(1)} %get-tuple-element.32, f32[8,32]{1,0:T(8,128)S(1)} %negate_multiply_fusion.2), kind=kOutput, calls=%fused_computation.13 | convolution fusion | flops 21540864 | bytes 333568 | tf_op jit(solution)/shard_map/transpose(jvp())/conv_general_dilated | solution.py:54
  255.2 6.5 collective-permute-start.15
  261.7 2.4 collective-permute-start.31
  264.2 37.5 %all-reduce = bf16[3,32,128]{2,1,0:T(8,128)(2,1)S(1)} all-reduce(bf16[3,32,128]{2,1,0:T(8,128)(2,1)S(1)} %convert_element_type.225), channel_id=2, replica_groups=mesh['dp'=64,'strip'=4] {'strip'}, use_global_device_ids=true, to_apply=%region_19.20.clone | all-reduce | flops 12288 | bytes 49152
  304.4 8.2 collective-permute-start.9
  315.6 2.6 collective-permute-start.6
  318.2 5.5 collective-permute-start.5
  325.1 297.3 %all-reduce.14 = (f32[3,8,128]{2,1,0:T(8,128)S(1)}, bf16[48,192]{0,1:T(8,128)(2,1)S(1)}, bf16[49,192]{0,1:T(8,128)(2,1)S(1)}, bf16[384,62]{1,0:T(8,128)(2,1)S(1)}) all-reduce(f32[3,8,128]{2,1,0:T(8,128)S(1)} %dynamic-slice_convert_fusion.3, f32[48,192]{0,1:T(8,128)S(1)} %convolution_bitcast_fusion.4, ...), channel_id=1, replica_groups=mesh['dp'=64,'strip'=4] {'dp'}, use_global_device_ids=true, to_apply=%region_20.21 | all-reduce | flops 45504 | bytes 279168 | tf_op jit(solution)/shard_map/psum | solution.py:225
  625.0 1.9 collective-permute-start.1
  627.0 1.9 collective-permute-start
  630.8 62.3 %psum.57 = f32[]{:T(128)} all-reduce(f32[]{:T(128)} %multiply_reduce_fusion.3), channel_id=1, replica_groups=mesh['dp'=64,'strip'=4] {'strip'}, use_global_device_ids=true, to_apply=%region_22.23 | all-reduce | flops 1 | bytes 8 | tf_op jit(solution)/shard_map/psum | solution.py:226
  693.8 10.8 %collective-permute-start.29 = (bf16[16,192]{1,0:T(8,128)(2,1)S(1)}, bf16[16,192]{1,0:T(8,128)(2,1)S(1)}, u32[]{:S(2)}, u32[]{:S(2)}) collective-permute-start(bf16[16,192]{1,0:T(8,128)(2,1)S(1)} %convert.107), channel_id=1, source_target_pairs={{0,56},{4,60},{8,64},{12,68},{16,72},{20,76},{24,80},{28,84},{32,8... | collective-permute-start | bytes 18440
  704.6 2.8 collective-permute-start.28
  707.5 10.6 %collective-permute-start.27 = (bf16[16,192]{1,0:T(8,128)(2,1)S(1)}, bf16[16,192]{1,0:T(8,128)(2,1)S(1)}, u32[]{:S(2)}, u32[]{:S(2)}) collective-permute-start(bf16[16,192]{1,0:T(8,128)(2,1)S(1)} %convert.107), channel_id=1, source_target_pairs={{0,48},{4,52},{8,56},{12,60},{16,64},{20,68},{24,72},{28,76},{32,8... | collective-permute-start | bytes 18440
  718.1 5.8 collective-permute-start.26
  727.3 2.3 collective-permute-start.23
  729.5 3.4 collective-permute-start.22
  733.0 4.0 collective-permute-start.21
  737.0 2.5 collective-permute-start.20
  739.6 2.5 collective-permute-start.19
  742.1 3.1 collective-permute-start.18
  745.3 3.1 collective-permute-start.17
  748.3 3.1 collective-permute-start.16
  754.1 2.0 collective-permute-start.45
  756.1 3.1 collective-permute-start.44
  763.6 1.9 concatenate
  765.5 1.9 collective-permute-start.41
  767.4 3.1 collective-permute-start.40
  771.9 3.4 collective-permute-start.38
  775.3 2.3 collective-permute-start.37
  777.7 1.9 concatenate.1
  779.6 2.7 collective-permute-start.36
  782.4 2.5 collective-permute-start.35
  784.9 3.5 collective-permute-start.34
  788.4 3.4 collective-permute-start.33
  791.8 3.1 collective-permute-start.32
  795.0 3.7 collective-permute-done.32
  798.6 1.8 concatenate.2
  800.5 15.9 %all-reduce.11 = (bf16[48,3]{0,1:T(4,128)(2,1)S(1)}, bf16[49,3]{0,1:T(4,128)(2,1)S(1)}, bf16[192,12]{0,1:T(8,128)(2,1)S(1)}, bf16[12,192]{1,0:T(8,128)(2,1)S(1)}...) all-reduce(bf16[48,3]{0,1:T(4,128)(2,1)S(1)} %dynamic-slice_convert, ...), channel_id=1, replica_groups=mesh['dp'=64,'strip'=4] {'strip'}, use_global_device_ids=true, to_apply=%region_26.27 | all-reduce | flops 9879 | bytes 39516 | tf_op jit(solution)/shard_map/psum | solution.py:216
  (229 shorter events, 56.1 us)
Async XLA Ops:
  0.6 20.2 %all-to-all-start = ((bf16[4,3,8,128]{3,2,1,0:T(8,128)(2,1)}), bf16[4,3,8,128]{3,2,1,0:T(8,128)(2,1)S(1)}, u32[]{:S(2)}, u32[]{:S(2)}) async-start(bf16[4,3,8,128]{3,2,1,0:T(8,128)(2,1)} %param.15), calls=%async_computation | async-start | bytes 49152 | tf_op jit(solution)/shard_map/all_to_all | solution.py:175
  230.3 74.0 %collective-permute-start.14 = (bf16[192,16]{0,1:T(8,128)(2,1)S(1)}, bf16[192,16]{0,1:T(8,128)(2,1)S(1)}, u32[]{:S(2)}, u32[]{:S(2)}) collective-permute-start(bf16[192,16]{0,1:T(8,128)(2,1)S(1)} %convert.108), channel_id=1, source_target_pairs={{0,60},{4,64},{8,68},{12,72},{16,76},{20,80},{24,84},{28,88},{32,9... | collective-permute-start | bytes 18440
  231.8 81.0 %collective-permute-start.13 = (bf16[192,16]{0,1:T(8,128)(2,1)S(1)}, bf16[192,16]{0,1:T(8,128)(2,1)S(1)}, u32[]{:S(2)}, u32[]{:S(2)}) collective-permute-start(bf16[192,16]{0,1:T(8,128)(2,1)S(1)} %convert.108), channel_id=1, source_target_pairs={{0,56},{4,60},{8,64},{12,68},{16,72},{20,76},{24,80},{28,84},{32,8... | collective-permute-start | bytes 18440
  236.0 78.3 %collective-permute-start.12 = (bf16[192,16]{0,1:T(8,128)(2,1)S(1)}, bf16[192,16]{0,1:T(8,128)(2,1)S(1)}, u32[]{:S(2)}, u32[]{:S(2)}) collective-permute-start(bf16[192,16]{0,1:T(8,128)(2,1)S(1)} %convert.108), channel_id=1, source_target_pairs={{0,52},{4,56},{8,60},{12,64},{16,68},{20,72},{24,76},{28,80},{32,8... | collective-permute-start | bytes 18440
  255.2 46.6 %collective-permute-start.15 = (bf16[192,12]{0,1:T(8,128)(2,1)S(1)}, bf16[192,12]{0,1:T(8,128)(2,1)S(1)}, u32[]{:S(2)}, u32[]{:S(2)}) collective-permute-start(bf16[192,12]{0,1:T(8,128)(2,1)S(1)} %slice), channel_id=1, source_target_pairs={{0,64},{4,68},{8,72},{12,76},{16,80},{20,84},{24,88},{28,92},{32,9... | collective-permute-start | bytes 13832
  261.7 41.4 %collective-permute-start.31 = (bf16[12,192]{1,0:T(8,128)(2,1)S(1)}, bf16[12,192]{1,0:T(8,128)(2,1)S(1)}, u32[]{:S(2)}, u32[]{:S(2)}) collective-permute-start(bf16[12,192]{1,0:T(8,128)(2,1)S(1)} %slice.1), channel_id=1, source_target_pairs={{0,64},{4,68},{8,72},{12,76},{16,80},{20,84},{24,88},{28,92},{32,9... | collective-permute-start | bytes 13832
  301.8 13.8 %collective-permute-start.11 = (bf16[192,16]{0,1:T(8,128)(2,1)S(1)}, bf16[192,16]{0,1:T(8,128)(2,1)S(1)}, u32[]{:S(2)}, u32[]{:S(2)}) collective-permute-start(bf16[192,16]{0,1:T(8,128)(2,1)S(1)} %convert.108), channel_id=1, source_target_pairs={{0,48},{4,52},{8,56},{12,60},{16,64},{20,68},{24,72},{28,76},{32,8... | collective-permute-start | bytes 18440
  303.1 15.2 %collective-permute-start.10 = (bf16[192,16]{0,1:T(8,128)(2,1)S(1)}, bf16[192,16]{0,1:T(8,128)(2,1)S(1)}, u32[]{:S(2)}, u32[]{:S(2)}) collective-permute-start(bf16[192,16]{0,1:T(8,128)(2,1)S(1)} %convert.108), channel_id=1, source_target_pairs={{0,44},{4,48},{8,52},{12,56},{16,60},{20,64},{24,68},{28,72},{32,7... | collective-permute-start | bytes 18440
  304.4 19.4 %collective-permute-start.9 = (bf16[192,16]{0,1:T(8,128)(2,1)S(1)}, bf16[192,16]{0,1:T(8,128)(2,1)S(1)}, u32[]{:S(2)}, u32[]{:S(2)}) collective-permute-start(bf16[192,16]{0,1:T(8,128)(2,1)S(1)} %convert.108), channel_id=1, source_target_pairs={{0,40},{4,44},{8,48},{12,52},{16,56},{20,60},{24,64},{28,68},{32,7... | collective-permute-start | bytes 18440
  312.7 309.7 %collective-permute-start.8 = (bf16[192,16]{0,1:T(8,128)(2,1)S(1)}, bf16[192,16]{0,1:T(8,128)(2,1)S(1)}, u32[]{:S(2)}, u32[]{:S(2)}) collective-permute-start(bf16[192,16]{0,1:T(8,128)(2,1)S(1)} %convert.108), channel_id=1, source_target_pairs={{0,36},{4,40},{8,44},{12,48},{16,52},{20,56},{24,60},{28,64},{32,6... | collective-permute-start | bytes 18440
  314.3 309.5 %collective-permute-start.7 = (bf16[192,16]{0,1:T(8,128)(2,1)S(1)}, bf16[192,16]{0,1:T(8,128)(2,1)S(1)}, u32[]{:S(2)}, u32[]{:S(2)}) collective-permute-start(bf16[192,16]{0,1:T(8,128)(2,1)S(1)} %convert.108), channel_id=1, source_target_pairs={{0,32},{4,36},{8,40},{12,44},{16,48},{20,52},{24,56},{28,60},{32,6... | collective-permute-start | bytes 18440
  315.6 309.5 %collective-permute-start.6 = (bf16[192,16]{0,1:T(8,128)(2,1)S(1)}, bf16[192,16]{0,1:T(8,128)(2,1)S(1)}, u32[]{:S(2)}, u32[]{:S(2)}) collective-permute-start(bf16[192,16]{0,1:T(8,128)(2,1)S(1)} %convert.108), channel_id=1, source_target_pairs={{0,28},{4,32},{8,36},{12,40},{16,44},{20,48},{24,52},{28,56},{32,6... | collective-permute-start | bytes 18440
  318.2 308.7 %collective-permute-start.5 = (bf16[192,16]{0,1:T(8,128)(2,1)S(1)}, bf16[192,16]{0,1:T(8,128)(2,1)S(1)}, u32[]{:S(2)}, u32[]{:S(2)}) collective-permute-start(bf16[192,16]{0,1:T(8,128)(2,1)S(1)} %convert.108), channel_id=1, source_target_pairs={{0,24},{4,28},{8,32},{12,36},{16,40},{20,44},{24,48},{28,52},{32,5... | collective-permute-start | bytes 18440
  323.8 305.2 %collective-permute-start.4 = (bf16[192,16]{0,1:T(8,128)(2,1)S(1)}, bf16[192,16]{0,1:T(8,128)(2,1)S(1)}, u32[]{:S(2)}, u32[]{:S(2)}) collective-permute-start(bf16[192,16]{0,1:T(8,128)(2,1)S(1)} %convert.108), channel_id=1, source_target_pairs={{0,20},{4,24},{8,28},{12,32},{16,36},{20,40},{24,44},{28,48},{32,5... | collective-permute-start | bytes 18440
  622.4 71.4 %collective-permute-start.3 = (bf16[192,16]{0,1:T(8,128)(2,1)S(1)}, bf16[192,16]{0,1:T(8,128)(2,1)S(1)}, u32[]{:S(2)}, u32[]{:S(2)}) collective-permute-start(bf16[192,16]{0,1:T(8,128)(2,1)S(1)} %convert.108), channel_id=1, source_target_pairs={{0,16},{4,20},{8,24},{12,28},{16,32},{20,36},{24,40},{28,44},{32,4... | collective-permute-start | bytes 18440
  623.7 80.9 %collective-permute-start.2 = (bf16[192,16]{0,1:T(8,128)(2,1)S(1)}, bf16[192,16]{0,1:T(8,128)(2,1)S(1)}, u32[]{:S(2)}, u32[]{:S(2)}) collective-permute-start(bf16[192,16]{0,1:T(8,128)(2,1)S(1)} %convert.108), channel_id=1, source_target_pairs={{0,12},{4,16},{8,20},{12,24},{16,28},{20,32},{24,36},{28,40},{32,4... | collective-permute-start | bytes 18440
  625.0 82.4 %collective-permute-start.1 = (bf16[192,16]{0,1:T(8,128)(2,1)S(1)}, bf16[192,16]{0,1:T(8,128)(2,1)S(1)}, u32[]{:S(2)}, u32[]{:S(2)}) collective-permute-start(bf16[192,16]{0,1:T(8,128)(2,1)S(1)} %convert.108), channel_id=1, source_target_pairs={{0,8},{4,12},{8,16},{12,20},{16,24},{20,28},{24,32},{28,36},{32,40... | collective-permute-start | bytes 18440
  627.0 91.1 %collective-permute-start = (bf16[192,16]{0,1:T(8,128)(2,1)S(1)}, bf16[192,16]{0,1:T(8,128)(2,1)S(1)}, u32[]{:S(2)}, u32[]{:S(2)}) collective-permute-start(bf16[192,16]{0,1:T(8,128)(2,1)S(1)} %convert.108), channel_id=1, source_target_pairs={{0,4},{4,8},{8,12},{12,16},{16,20},{20,24},{24,28},{28,32},{32,36}... | collective-permute-start | bytes 18440
  628.9 95.0 %collective-permute-start.30 = (bf16[16,192]{1,0:T(8,128)(2,1)S(1)}, bf16[16,192]{1,0:T(8,128)(2,1)S(1)}, u32[]{:S(2)}, u32[]{:S(2)}) collective-permute-start(bf16[16,192]{1,0:T(8,128)(2,1)S(1)} %convert.107), channel_id=1, source_target_pairs={{0,60},{4,64},{8,68},{12,72},{16,76},{20,80},{24,84},{28,88},{32,9... | collective-permute-start | bytes 18440
  693.8 32.1 %collective-permute-start.29 = (bf16[16,192]{1,0:T(8,128)(2,1)S(1)}, bf16[16,192]{1,0:T(8,128)(2,1)S(1)}, u32[]{:S(2)}, u32[]{:S(2)}) collective-permute-start(bf16[16,192]{1,0:T(8,128)(2,1)S(1)} %convert.107), channel_id=1, source_target_pairs={{0,56},{4,60},{8,64},{12,68},{16,72},{20,76},{24,80},{28,84},{32,8... | collective-permute-start | bytes 18440
  704.6 22.6 %collective-permute-start.28 = (bf16[16,192]{1,0:T(8,128)(2,1)S(1)}, bf16[16,192]{1,0:T(8,128)(2,1)S(1)}, u32[]{:S(2)}, u32[]{:S(2)}) collective-permute-start(bf16[16,192]{1,0:T(8,128)(2,1)S(1)} %convert.107), channel_id=1, source_target_pairs={{0,52},{4,56},{8,60},{12,64},{16,68},{20,72},{24,76},{28,80},{32,8... | collective-permute-start | bytes 18440
  707.5 22.0 %collective-permute-start.27 = (bf16[16,192]{1,0:T(8,128)(2,1)S(1)}, bf16[16,192]{1,0:T(8,128)(2,1)S(1)}, u32[]{:S(2)}, u32[]{:S(2)}) collective-permute-start(bf16[16,192]{1,0:T(8,128)(2,1)S(1)} %convert.107), channel_id=1, source_target_pairs={{0,48},{4,52},{8,56},{12,60},{16,64},{20,68},{24,72},{28,76},{32,8... | collective-permute-start | bytes 18440
  718.1 14.9 %collective-permute-start.26 = (bf16[16,192]{1,0:T(8,128)(2,1)S(1)}, bf16[16,192]{1,0:T(8,128)(2,1)S(1)}, u32[]{:S(2)}, u32[]{:S(2)}) collective-permute-start(bf16[16,192]{1,0:T(8,128)(2,1)S(1)} %convert.107), channel_id=1, source_target_pairs={{0,44},{4,48},{8,52},{12,56},{16,60},{20,64},{24,68},{28,72},{32,7... | collective-permute-start | bytes 18440
  724.0 13.0 %collective-permute-start.25 = (bf16[16,192]{1,0:T(8,128)(2,1)S(1)}, bf16[16,192]{1,0:T(8,128)(2,1)S(1)}, u32[]{:S(2)}, u32[]{:S(2)}) collective-permute-start(bf16[16,192]{1,0:T(8,128)(2,1)S(1)} %convert.107), channel_id=1, source_target_pairs={{0,40},{4,44},{8,48},{12,52},{16,56},{20,60},{24,64},{28,68},{32,7... | collective-permute-start | bytes 18440
  726.0 13.6 %collective-permute-start.24 = (bf16[16,192]{1,0:T(8,128)(2,1)S(1)}, bf16[16,192]{1,0:T(8,128)(2,1)S(1)}, u32[]{:S(2)}, u32[]{:S(2)}) collective-permute-start(bf16[16,192]{1,0:T(8,128)(2,1)S(1)} %convert.107), channel_id=1, source_target_pairs={{0,36},{4,40},{8,44},{12,48},{16,52},{20,56},{24,60},{28,64},{32,6... | collective-permute-start | bytes 18440
  727.3 14.8 %collective-permute-start.23 = (bf16[16,192]{1,0:T(8,128)(2,1)S(1)}, bf16[16,192]{1,0:T(8,128)(2,1)S(1)}, u32[]{:S(2)}, u32[]{:S(2)}) collective-permute-start(bf16[16,192]{1,0:T(8,128)(2,1)S(1)} %convert.107), channel_id=1, source_target_pairs={{0,32},{4,36},{8,40},{12,44},{16,48},{20,52},{24,56},{28,60},{32,6... | collective-permute-start | bytes 18440
  729.5 15.7 %collective-permute-start.22 = (bf16[16,192]{1,0:T(8,128)(2,1)S(1)}, bf16[16,192]{1,0:T(8,128)(2,1)S(1)}, u32[]{:S(2)}, u32[]{:S(2)}) collective-permute-start(bf16[16,192]{1,0:T(8,128)(2,1)S(1)} %convert.107), channel_id=1, source_target_pairs={{0,28},{4,32},{8,36},{12,40},{16,44},{20,48},{24,52},{28,56},{32,6... | collective-permute-start | bytes 18440
  733.0 15.4 %collective-permute-start.21 = (bf16[16,192]{1,0:T(8,128)(2,1)S(1)}, bf16[16,192]{1,0:T(8,128)(2,1)S(1)}, u32[]{:S(2)}, u32[]{:S(2)}) collective-permute-start(bf16[16,192]{1,0:T(8,128)(2,1)S(1)} %convert.107), channel_id=1, source_target_pairs={{0,24},{4,28},{8,32},{12,36},{16,40},{20,44},{24,48},{28,52},{32,5... | collective-permute-start | bytes 18440
  737.0 14.5 %collective-permute-start.20 = (bf16[16,192]{1,0:T(8,128)(2,1)S(1)}, bf16[16,192]{1,0:T(8,128)(2,1)S(1)}, u32[]{:S(2)}, u32[]{:S(2)}) collective-permute-start(bf16[16,192]{1,0:T(8,128)(2,1)S(1)} %convert.107), channel_id=1, source_target_pairs={{0,20},{4,24},{8,28},{12,32},{16,36},{20,40},{24,44},{28,48},{32,5... | collective-permute-start | bytes 18440
  739.6 13.2 %collective-permute-start.19 = (bf16[16,192]{1,0:T(8,128)(2,1)S(1)}, bf16[16,192]{1,0:T(8,128)(2,1)S(1)}, u32[]{:S(2)}, u32[]{:S(2)}) collective-permute-start(bf16[16,192]{1,0:T(8,128)(2,1)S(1)} %convert.107), channel_id=1, source_target_pairs={{0,16},{4,20},{8,24},{12,28},{16,32},{20,36},{24,40},{28,44},{32,4... | collective-permute-start | bytes 18440
  742.1 12.0 %collective-permute-start.18 = (bf16[16,192]{1,0:T(8,128)(2,1)S(1)}, bf16[16,192]{1,0:T(8,128)(2,1)S(1)}, u32[]{:S(2)}, u32[]{:S(2)}) collective-permute-start(bf16[16,192]{1,0:T(8,128)(2,1)S(1)} %convert.107), channel_id=1, source_target_pairs={{0,12},{4,16},{8,20},{12,24},{16,28},{20,32},{24,36},{28,40},{32,4... | collective-permute-start | bytes 18440
  745.3 10.9 %collective-permute-start.17 = (bf16[16,192]{1,0:T(8,128)(2,1)S(1)}, bf16[16,192]{1,0:T(8,128)(2,1)S(1)}, u32[]{:S(2)}, u32[]{:S(2)}) collective-permute-start(bf16[16,192]{1,0:T(8,128)(2,1)S(1)} %convert.107), channel_id=1, source_target_pairs={{0,8},{4,12},{8,16},{12,20},{16,24},{20,28},{24,32},{28,36},{32,40... | collective-permute-start | bytes 18440
  748.3 10.9 %collective-permute-start.16 = (bf16[16,192]{1,0:T(8,128)(2,1)S(1)}, bf16[16,192]{1,0:T(8,128)(2,1)S(1)}, u32[]{:S(2)}, u32[]{:S(2)}) collective-permute-start(bf16[16,192]{1,0:T(8,128)(2,1)S(1)} %convert.107), channel_id=1, source_target_pairs={{0,4},{4,8},{8,12},{12,16},{16,20},{20,24},{24,28},{28,32},{32,36}... | collective-permute-start | bytes 18440
  751.5 9.2 %collective-permute-start.47 = (bf16[768,6]{0,1:T(8,128)(2,1)S(1)}, bf16[768,6]{0,1:T(8,128)(2,1)S(1)}, u32[]{:S(2)}, u32[]{:S(2)}) collective-permute-start(bf16[768,6]{0,1:T(8,128)(2,1)S(1)} %slice.2), channel_id=1, source_target_pairs={{0,64},{4,68},{8,72},{12,76},{16,80},{20,84},{24,88},{28,92},{32,9... | collective-permute-start | bytes 27656
  752.8 12.7 %collective-permute-start.46 = (bf16[768,8]{0,1:T(8,128)(2,1)S(1)}, bf16[768,8]{0,1:T(8,128)(2,1)S(1)}, u32[]{:S(2)}, u32[]{:S(2)}) collective-permute-start(bf16[768,8]{0,1:T(8,128)(2,1)S(1)} %convert.106), channel_id=1, source_target_pairs={{0,60},{4,64},{8,68},{12,72},{16,76},{20,80},{24,84},{28,88},{32,9... | collective-permute-start | bytes 36872
  754.1 13.3 %collective-permute-start.45 = (bf16[768,8]{0,1:T(8,128)(2,1)S(1)}, bf16[768,8]{0,1:T(8,128)(2,1)S(1)}, u32[]{:S(2)}, u32[]{:S(2)}) collective-permute-start(bf16[768,8]{0,1:T(8,128)(2,1)S(1)} %convert.106), channel_id=1, source_target_pairs={{0,56},{4,60},{8,64},{12,68},{16,72},{20,76},{24,80},{28,84},{32,8... | collective-permute-start | bytes 36872
  756.1 14.4 %collective-permute-start.44 = (bf16[768,8]{0,1:T(8,128)(2,1)S(1)}, bf16[768,8]{0,1:T(8,128)(2,1)S(1)}, u32[]{:S(2)}, u32[]{:S(2)}) collective-permute-start(bf16[768,8]{0,1:T(8,128)(2,1)S(1)} %convert.106), channel_id=1, source_target_pairs={{0,52},{4,56},{8,60},{12,64},{16,68},{20,72},{24,76},{28,80},{32,8... | collective-permute-start | bytes 36872
  759.3 12.6 %collective-permute-start.43 = (bf16[768,8]{0,1:T(8,128)(2,1)S(1)}, bf16[768,8]{0,1:T(8,128)(2,1)S(1)}, u32[]{:S(2)}, u32[]{:S(2)}) collective-permute-start(bf16[768,8]{0,1:T(8,128)(2,1)S(1)} %convert.106), channel_id=1, source_target_pairs={{0,48},{4,52},{8,56},{12,60},{16,64},{20,68},{24,72},{28,76},{32,8... | collective-permute-start | bytes 36872
  760.7 14.7 %collective-permute-start.42 = (bf16[768,8]{0,1:T(8,128)(2,1)S(1)}, bf16[768,8]{0,1:T(8,128)(2,1)S(1)}, u32[]{:S(2)}, u32[]{:S(2)}) collective-permute-start(bf16[768,8]{0,1:T(8,128)(2,1)S(1)} %convert.106), channel_id=1, source_target_pairs={{0,44},{4,48},{8,52},{12,56},{16,60},{20,64},{24,68},{28,72},{32,7... | collective-permute-start | bytes 36872
  765.5 14.1 %collective-permute-start.41 = (bf16[768,8]{0,1:T(8,128)(2,1)S(1)}, bf16[768,8]{0,1:T(8,128)(2,1)S(1)}, u32[]{:S(2)}, u32[]{:S(2)}) collective-permute-start(bf16[768,8]{0,1:T(8,128)(2,1)S(1)} %convert.106), channel_id=1, source_target_pairs={{0,40},{4,44},{8,48},{12,52},{16,56},{20,60},{24,64},{28,68},{32,7... | collective-permute-start | bytes 36872
  767.4 14.9 %collective-permute-start.40 = (bf16[768,8]{0,1:T(8,128)(2,1)S(1)}, bf16[768,8]{0,1:T(8,128)(2,1)S(1)}, u32[]{:S(2)}, u32[]{:S(2)}) collective-permute-start(bf16[768,8]{0,1:T(8,128)(2,1)S(1)} %convert.106), channel_id=1, source_target_pairs={{0,36},{4,40},{8,44},{12,48},{16,52},{20,56},{24,60},{28,64},{32,6... | collective-permute-start | bytes 36872
  770.6 14.3 %collective-permute-start.39 = (bf16[768,8]{0,1:T(8,128)(2,1)S(1)}, bf16[768,8]{0,1:T(8,128)(2,1)S(1)}, u32[]{:S(2)}, u32[]{:S(2)}) collective-permute-start(bf16[768,8]{0,1:T(8,128)(2,1)S(1)} %convert.106), channel_id=1, source_target_pairs={{0,32},{4,36},{8,40},{12,44},{16,48},{20,52},{24,56},{28,60},{32,6... | collective-permute-start | bytes 36872
  771.9 16.5 %collective-permute-start.38 = (bf16[768,8]{0,1:T(8,128)(2,1)S(1)}, bf16[768,8]{0,1:T(8,128)(2,1)S(1)}, u32[]{:S(2)}, u32[]{:S(2)}) collective-permute-start(bf16[768,8]{0,1:T(8,128)(2,1)S(1)} %convert.106), channel_id=1, source_target_pairs={{0,28},{4,32},{8,36},{12,40},{16,44},{20,48},{24,52},{28,56},{32,6... | collective-permute-start | bytes 36872
  775.3 16.4 %collective-permute-start.37 = (bf16[768,8]{0,1:T(8,128)(2,1)S(1)}, bf16[768,8]{0,1:T(8,128)(2,1)S(1)}, u32[]{:S(2)}, u32[]{:S(2)}) collective-permute-start(bf16[768,8]{0,1:T(8,128)(2,1)S(1)} %convert.106), channel_id=1, source_target_pairs={{0,24},{4,28},{8,32},{12,36},{16,40},{20,44},{24,48},{28,52},{32,5... | collective-permute-start | bytes 36872
  779.6 15.3 %collective-permute-start.36 = (bf16[768,8]{0,1:T(8,128)(2,1)S(1)}, bf16[768,8]{0,1:T(8,128)(2,1)S(1)}, u32[]{:S(2)}, u32[]{:S(2)}) collective-permute-start(bf16[768,8]{0,1:T(8,128)(2,1)S(1)} %convert.106), channel_id=1, source_target_pairs={{0,20},{4,24},{8,28},{12,32},{16,36},{20,40},{24,44},{28,48},{32,5... | collective-permute-start | bytes 36872
  782.4 12.6 %collective-permute-start.35 = (bf16[768,8]{0,1:T(8,128)(2,1)S(1)}, bf16[768,8]{0,1:T(8,128)(2,1)S(1)}, u32[]{:S(2)}, u32[]{:S(2)}) collective-permute-start(bf16[768,8]{0,1:T(8,128)(2,1)S(1)} %convert.106), channel_id=1, source_target_pairs={{0,16},{4,20},{8,24},{12,28},{16,32},{20,36},{24,40},{28,44},{32,4... | collective-permute-start | bytes 36872
  784.9 10.1 %collective-permute-start.34 = (bf16[768,8]{0,1:T(8,128)(2,1)S(1)}, bf16[768,8]{0,1:T(8,128)(2,1)S(1)}, u32[]{:S(2)}, u32[]{:S(2)}) collective-permute-start(bf16[768,8]{0,1:T(8,128)(2,1)S(1)} %convert.106), channel_id=1, source_target_pairs={{0,12},{4,16},{8,20},{12,24},{16,28},{20,32},{24,36},{28,40},{32,4... | collective-permute-start | bytes 36872
  791.8 6.8 collective-permute-start.32
  (35 other events, 1130.6 us)
where the time goes:
time: 823 us; the launch traced here: 821 us
  blocking collectives  597 us (73%)
  starting transfers between devices  146 us (18%)
  matrix products  25.1 us (3%)
  local copies, waits for them, and re-layouts  18.1 us (2%)
  other arithmetic  17.8 us (2%)
  between operations  13.3 us (2%)
    psum x1, blocking collectives, on_device(): summed_delta = lax.psum(delta_part, 'dp')  297 us
    unnamed x2, blocking collectives  216 us
    unnamed x48, starting transfers between devices  142 us
    psum x1, blocking collectives, on_device(): squares = lax.psum(jnp.sum(summed_delta * summed_delta), 'strip')  62.3 us
  transfers between devices with their start and end apart: 49, of which 1 were waited for; matrix products, arithmetic and copies ran while one was open for 4% of the time, Pallas kernels for 0%

commit v1 on v0

--- a/solution.py
+++ b/solution.py
@@ -222,7 +222,7 @@
     )
     stem_grad, dw1_grad, up1_grad, down1_grad, ds_grad, head_grad = summed
     levels = STEP_UNIT * step_levels.astype(jnp.float32)
-    summed_delta = lax.psum(delta_part, "dp")
+    summed_delta = jnp.sum(lax.all_gather(delta_part, "dp"), axis=0)
     squares = lax.psum(jnp.sum(summed_delta * summed_delta), "strip")
     cells = delta_part.size * lax.axis_size("strip")
     spread = jnp.sqrt(squares / cells + EPS_ROOT)

time: 823 us -> 999 us (1.21)
  blocking collectives: 597 us -> 765 us
    unnamed x2 -> x3, blocking collectives: 216 us -> 578 us
    psum x2 -> x0, blocking collectives: 313 us -> none  [the longest x1 297 us: on_device(): summed_delta = lax.psum(delta_part, 'dp')]
    all_gather x0 -> x1, blocking collectives: none -> 148 us  [on_device(): summed_delta = jnp.sum(lax.all_gather(delta_part, 'dp'), axis=0)]
    psum x1, blocking collectives: 62.3 us -> 33.4 us  [on_device(): squares = lax.psum(jnp.sum(summed_delta * summed_delta), 'strip')]
  transfers between devices with their start and end apart: 49 -> 49, of which waited for: 1 -> 1; matrix products, arithmetic and copies ran while one was open for 4% -> 3% of each run, Pallas kernels for 0% -> 0%
where the time goes in v1:
time: 999 us; the launch traced here: 991 us
  blocking collectives  765 us (77%)
  starting transfers between devices  148 us (15%)
  matrix products  24.9 us (2%)
  local copies, waits for them, and re-layouts  18.1 us (2%)
  other arithmetic  17.9 us (2%)
  between operations  13.3 us (1%)
    unnamed x3, blocking collectives  578 us
    all_gather x1, blocking collectives, on_device(): summed_delta = jnp.sum(lax.all_gather(delta_part, 'dp'), axis=0)  148 us
    unnamed x48, starting transfers between devices  144 us
    psum x1, blocking collectives, on_device(): squares = lax.psum(jnp.sum(summed_delta * summed_delta), 'strip')  33.4 us
  transfers between devices with their start and end apart: 49, of which 1 were waited for; matrix products, arithmetic and copies ran while one was open for 3% of the time, Pallas kernels for 0%

profile of v1, /device:TPU:9, one launch (start us, length us, event | category | flops | bytes accessed | tf_op | source)
XLA Modules:
  0.0 991.2 jit_solution(11049276492576146029)
XLA Ops:
  0.6 4.0 all-to-all-start
  15.5 5.4 all_gather.12
  20.9 1.7 convert_element_type.198
  24.2 4.8 fusion.63
  30.6 2.8 multiply_convert_fusion
  41.4 1.8 fusion.53
  51.4 178.9 %fusion.51 = (f32[192,16]{0,1:T(8,128)S(1)}, f32[16,192]{1,0:T(8,128)S(1)}, f32[768,8]{0,1:T(8,128)S(1)}) fusion(f32[192,768]{0,1:T(8,128)S(1)} %convolution_bitcast_fusion.2, f32[768,192]{1,0:T(8,128)} %convolution_bitcast_fusion.1, f32[768,384]{0,1:T(8,128)S(1)} %convolution_bitcast_fusion), kind=kCustom, calls=%all-reduce-scatter.3 | all-reduce-scatter fusion | flops 786434 | bytes 2409472
  231.6 4.5 collective-permute-start.13
  242.2 6.3 collective-permute-start.15
  248.5 2.5 collective-permute-start.31
  254.0 10.5 %collective-permute-start.9 = (bf16[192,16]{0,1:T(8,128)(2,1)S(1)}, bf16[192,16]{0,1:T(8,128)(2,1)S(1)}, u32[]{:S(2)}, u32[]{:S(2)}) collective-permute-start(bf16[192,16]{0,1:T(8,128)(2,1)S(1)} %convert.109), channel_id=1, source_target_pairs={{0,40},{4,44},{8,48},{12,52},{16,56},{20,60},{24,64},{28,68},{32,7... | collective-permute-start | bytes 18440
  264.5 9.7 convolution_reduce_fusion
  274.2 1.9 collective-permute-start.8
  277.4 4.9 collective-permute-start.6
  282.4 2.8 collective-permute-start.5
  285.2 2.8 collective-permute-start.4
  288.6 2.5 collective-permute-start.3
  291.2 4.0 collective-permute-start.2
  295.2 2.8 collective-permute-start.1
  298.0 3.1 collective-permute-start
  304.5 3.8 collective-permute-start.28
  312.5 297.8 %all-reduce.14 = (bf16[48,192]{0,1:T(8,128)(2,1)S(1)}, bf16[49,192]{0,1:T(8,128)(2,1)S(1)}, bf16[384,62]{1,0:T(8,128)(2,1)S(1)}) all-reduce(f32[48,192]{0,1:T(8,128)S(1)} %convolution_bitcast_fusion.4, f32[49,192]{0,1:T(8,128)S(1)} %copy.61, f32[384,62]{1,0:T(8,128)S(1)} %broadcast_multiply_fusion.1), channel_id=4, replica_groups=mesh['dp'=64,'strip'=4] {'dp'}, use_global_device_ids=true, to_apply=%region_25.26.clone | all-reduce | flops 42432 | bytes 254592
  614.3 12.1 %collective-permute-start.21 = (bf16[16,192]{1,0:T(8,128)(2,1)S(1)}, bf16[16,192]{1,0:T(8,128)(2,1)S(1)}, u32[]{:S(2)}, u32[]{:S(2)}) collective-permute-start(bf16[16,192]{1,0:T(8,128)(2,1)S(1)} %convert.108), channel_id=1, source_target_pairs={{0,24},{4,28},{8,32},{12,36},{16,40},{20,44},{24,48},{28,52},{32,5... | collective-permute-start | bytes 18440
  627.8 3.1 collective-permute-start.19
  630.9 4.9 collective-permute-start.18
  635.8 3.7 collective-permute-start.17
  639.6 3.1 collective-permute-start.16
  642.7 5.7 collective-permute-start.47
  648.4 4.4 collective-permute-start.46
  652.8 2.3 collective-permute-start.45
  655.1 1.9 collective-permute-start.44
  657.0 2.8 collective-permute-start.43
  659.8 2.5 collective-permute-start.42
  665.2 1.9 concatenate
  668.4 3.4 collective-permute-start.40
  673.2 3.1 collective-permute-start.38
  676.3 2.6 collective-permute-start.37
  678.9 1.9 concatenate.1
  680.9 3.1 collective-permute-start.36
  684.0 2.5 collective-permute-start.35
  686.5 3.1 collective-permute-start.34
  689.6 2.8 collective-permute-start.33
  692.4 2.9 collective-permute-start.32
  695.4 3.9 collective-permute-done.32
  699.2 1.8 concatenate.2
  701.1 101.1 %all-reduce.11 = (bf16[3,32,128]{2,1,0:T(8,128)(2,1)S(1)}, bf16[48,3]{0,1:T(4,128)(2,1)S(1)}, bf16[49,3]{0,1:T(4,128)(2,1)S(1)}, bf16[192,12]{0,1:T(8,128)(2,1)S...) all-reduce(bf16[3,32,128]{2,1,0:T(8,128)(2,1)S(1)} %convert_element, ...), channel_id=3, replica_groups=mesh['dp'=64,'strip'=4] {'strip'}, use_global_device_ids=true, to_apply=%region_19.20.clone | all-reduce | flops 22167 | bytes 88668
  802.2 148.3 %all-gather = f32[192,8,128]{2,1,0:T(8,128)S(1)} all-gather(f32[3,8,128]{2,1,0:T(8,128)S(1)} %dynamic-slice_convert_fusion.3), channel_id=2, replica_groups=mesh['dp'=64,'strip'=4] {'dp'}, dimensions={0}, use_global_device_ids=true | all-gather | bytes 798720 | tf_op jit(solution)/shard_map/all_gather | solution.py:225
  951.8 33.4 %psum.49 = f32[]{:T(128)} all-reduce(f32[]{:T(128)} %multiply_reduce_fusion.3), channel_id=1, replica_groups=mesh['dp'=64,'strip'=4] {'strip'}, use_global_device_ids=true, to_apply=%region_22.23 | all-reduce | flops 1 | bytes 8 | tf_op jit(solution)/shard_map/psum | solution.py:226
  (230 shorter events, 56.4 us)
Async XLA Ops:
  0.6 20.3 %all-to-all-start = ((bf16[4,3,8,128]{3,2,1,0:T(8,128)(2,1)}), bf16[4,3,8,128]{3,2,1,0:T(8,128)(2,1)S(1)}, u32[]{:S(2)}, u32[]{:S(2)}) async-start(bf16[4,3,8,128]{3,2,1,0:T(8,128)(2,1)} %param.15), calls=%async_computation | async-start | bytes 49152 | tf_op jit(solution)/shard_map/all_to_all | solution.py:175
  230.3 23.7 %collective-permute-start.14 = (bf16[192,16]{0,1:T(8,128)(2,1)S(1)}, bf16[192,16]{0,1:T(8,128)(2,1)S(1)}, u32[]{:S(2)}, u32[]{:S(2)}) collective-permute-start(bf16[192,16]{0,1:T(8,128)(2,1)S(1)} %convert.109), channel_id=1, source_target_pairs={{0,60},{4,64},{8,68},{12,72},{16,76},{20,80},{24,84},{28,88},{32,9... | collective-permute-start | bytes 18440
  231.6 42.6 %collective-permute-start.13 = (bf16[192,16]{0,1:T(8,128)(2,1)S(1)}, bf16[192,16]{0,1:T(8,128)(2,1)S(1)}, u32[]{:S(2)}, u32[]{:S(2)}) collective-permute-start(bf16[192,16]{0,1:T(8,128)(2,1)S(1)} %convert.109), channel_id=1, source_target_pairs={{0,56},{4,60},{8,64},{12,68},{16,72},{20,76},{24,80},{28,84},{32,8... | collective-permute-start | bytes 18440
  236.1 40.0 %collective-permute-start.12 = (bf16[192,16]{0,1:T(8,128)(2,1)S(1)}, bf16[192,16]{0,1:T(8,128)(2,1)S(1)}, u32[]{:S(2)}, u32[]{:S(2)}) collective-permute-start(bf16[192,16]{0,1:T(8,128)(2,1)S(1)} %convert.109), channel_id=1, source_target_pairs={{0,52},{4,56},{8,60},{12,64},{16,68},{20,72},{24,76},{28,80},{32,8... | collective-permute-start | bytes 18440
  242.2 9.1 collective-permute-start.15
  251.3 26.2 %collective-permute-start.11 = (bf16[192,16]{0,1:T(8,128)(2,1)S(1)}, bf16[192,16]{0,1:T(8,128)(2,1)S(1)}, u32[]{:S(2)}, u32[]{:S(2)}) collective-permute-start(bf16[192,16]{0,1:T(8,128)(2,1)S(1)} %convert.109), channel_id=1, source_target_pairs={{0,48},{4,52},{8,56},{12,60},{16,64},{20,68},{24,72},{28,76},{32,8... | collective-permute-start | bytes 18440
  252.7 29.7 %collective-permute-start.10 = (bf16[192,16]{0,1:T(8,128)(2,1)S(1)}, bf16[192,16]{0,1:T(8,128)(2,1)S(1)}, u32[]{:S(2)}, u32[]{:S(2)}) collective-permute-start(bf16[192,16]{0,1:T(8,128)(2,1)S(1)} %convert.109), channel_id=1, source_target_pairs={{0,44},{4,48},{8,52},{12,56},{16,60},{20,64},{24,68},{28,72},{32,7... | collective-permute-start | bytes 18440
  254.0 31.2 %collective-permute-start.9 = (bf16[192,16]{0,1:T(8,128)(2,1)S(1)}, bf16[192,16]{0,1:T(8,128)(2,1)S(1)}, u32[]{:S(2)}, u32[]{:S(2)}) collective-permute-start(bf16[192,16]{0,1:T(8,128)(2,1)S(1)} %convert.109), channel_id=1, source_target_pairs={{0,40},{4,44},{8,48},{12,52},{16,56},{20,60},{24,64},{28,68},{32,7... | collective-permute-start | bytes 18440
  274.2 14.4 %collective-permute-start.8 = (bf16[192,16]{0,1:T(8,128)(2,1)S(1)}, bf16[192,16]{0,1:T(8,128)(2,1)S(1)}, u32[]{:S(2)}, u32[]{:S(2)}) collective-permute-start(bf16[192,16]{0,1:T(8,128)(2,1)S(1)} %convert.109), channel_id=1, source_target_pairs={{0,36},{4,40},{8,44},{12,48},{16,52},{20,56},{24,60},{28,64},{32,6... | collective-permute-start | bytes 18440
  276.1 15.0 %collective-permute-start.7 = (bf16[192,16]{0,1:T(8,128)(2,1)S(1)}, bf16[192,16]{0,1:T(8,128)(2,1)S(1)}, u32[]{:S(2)}, u32[]{:S(2)}) collective-permute-start(bf16[192,16]{0,1:T(8,128)(2,1)S(1)} %convert.109), channel_id=1, source_target_pairs={{0,32},{4,36},{8,40},{12,44},{16,48},{20,52},{24,56},{28,60},{32,6... | collective-permute-start | bytes 18440
  277.4 17.7 %collective-permute-start.6 = (bf16[192,16]{0,1:T(8,128)(2,1)S(1)}, bf16[192,16]{0,1:T(8,128)(2,1)S(1)}, u32[]{:S(2)}, u32[]{:S(2)}) collective-permute-start(bf16[192,16]{0,1:T(8,128)(2,1)S(1)} %convert.109), channel_id=1, source_target_pairs={{0,28},{4,32},{8,36},{12,40},{16,44},{20,48},{24,52},{28,56},{32,6... | collective-permute-start | bytes 18440
  282.4 15.6 %collective-permute-start.5 = (bf16[192,16]{0,1:T(8,128)(2,1)S(1)}, bf16[192,16]{0,1:T(8,128)(2,1)S(1)}, u32[]{:S(2)}, u32[]{:S(2)}) collective-permute-start(bf16[192,16]{0,1:T(8,128)(2,1)S(1)} %convert.109), channel_id=1, source_target_pairs={{0,24},{4,28},{8,32},{12,36},{16,40},{20,44},{24,48},{28,52},{32,5... | collective-permute-start | bytes 18440
  285.2 15.8 %collective-permute-start.4 = (bf16[192,16]{0,1:T(8,128)(2,1)S(1)}, bf16[192,16]{0,1:T(8,128)(2,1)S(1)}, u32[]{:S(2)}, u32[]{:S(2)}) collective-permute-start(bf16[192,16]{0,1:T(8,128)(2,1)S(1)} %convert.109), channel_id=1, source_target_pairs={{0,20},{4,24},{8,28},{12,32},{16,36},{20,40},{24,44},{28,48},{32,5... | collective-permute-start | bytes 18440
  288.6 14.5 %collective-permute-start.3 = (bf16[192,16]{0,1:T(8,128)(2,1)S(1)}, bf16[192,16]{0,1:T(8,128)(2,1)S(1)}, u32[]{:S(2)}, u32[]{:S(2)}) collective-permute-start(bf16[192,16]{0,1:T(8,128)(2,1)S(1)} %convert.109), channel_id=1, source_target_pairs={{0,16},{4,20},{8,24},{12,28},{16,32},{20,36},{24,40},{28,44},{32,4... | collective-permute-start | bytes 18440
  291.2 13.4 %collective-permute-start.2 = (bf16[192,16]{0,1:T(8,128)(2,1)S(1)}, bf16[192,16]{0,1:T(8,128)(2,1)S(1)}, u32[]{:S(2)}, u32[]{:S(2)}) collective-permute-start(bf16[192,16]{0,1:T(8,128)(2,1)S(1)} %convert.109), channel_id=1, source_target_pairs={{0,12},{4,16},{8,20},{12,24},{16,28},{20,32},{24,36},{28,40},{32,4... | collective-permute-start | bytes 18440
  295.2 13.1 %collective-permute-start.1 = (bf16[192,16]{0,1:T(8,128)(2,1)S(1)}, bf16[192,16]{0,1:T(8,128)(2,1)S(1)}, u32[]{:S(2)}, u32[]{:S(2)}) collective-permute-start(bf16[192,16]{0,1:T(8,128)(2,1)S(1)} %convert.109), channel_id=1, source_target_pairs={{0,8},{4,12},{8,16},{12,20},{16,24},{20,28},{24,32},{28,36},{32,40... | collective-permute-start | bytes 18440
  298.0 11.6 %collective-permute-start = (bf16[192,16]{0,1:T(8,128)(2,1)S(1)}, bf16[192,16]{0,1:T(8,128)(2,1)S(1)}, u32[]{:S(2)}, u32[]{:S(2)}) collective-permute-start(bf16[192,16]{0,1:T(8,128)(2,1)S(1)} %convert.109), channel_id=1, source_target_pairs={{0,4},{4,8},{8,12},{12,16},{16,20},{20,24},{24,28},{28,32},{32,36}... | collective-permute-start | bytes 18440
  301.1 10.1 %collective-permute-start.30 = (bf16[16,192]{1,0:T(8,128)(2,1)S(1)}, bf16[16,192]{1,0:T(8,128)(2,1)S(1)}, u32[]{:S(2)}, u32[]{:S(2)}) collective-permute-start(bf16[16,192]{1,0:T(8,128)(2,1)S(1)} %convert.108), channel_id=1, source_target_pairs={{0,60},{4,64},{8,68},{12,72},{16,76},{20,80},{24,84},{28,88},{32,9... | collective-permute-start | bytes 18440
  303.2 307.2 %collective-permute-start.29 = (bf16[16,192]{1,0:T(8,128)(2,1)S(1)}, bf16[16,192]{1,0:T(8,128)(2,1)S(1)}, u32[]{:S(2)}, u32[]{:S(2)}) collective-permute-start(bf16[16,192]{1,0:T(8,128)(2,1)S(1)} %convert.108), channel_id=1, source_target_pairs={{0,56},{4,60},{8,64},{12,68},{16,72},{20,76},{24,80},{28,84},{32,8... | collective-permute-start | bytes 18440
  304.5 307.2 %collective-permute-start.28 = (bf16[16,192]{1,0:T(8,128)(2,1)S(1)}, bf16[16,192]{1,0:T(8,128)(2,1)S(1)}, u32[]{:S(2)}, u32[]{:S(2)}) collective-permute-start(bf16[16,192]{1,0:T(8,128)(2,1)S(1)} %convert.108), channel_id=1, source_target_pairs={{0,52},{4,56},{8,60},{12,64},{16,68},{20,72},{24,76},{28,80},{32,8... | collective-permute-start | bytes 18440
  308.3 304.7 %collective-permute-start.27 = (bf16[16,192]{1,0:T(8,128)(2,1)S(1)}, bf16[16,192]{1,0:T(8,128)(2,1)S(1)}, u32[]{:S(2)}, u32[]{:S(2)}) collective-permute-start(bf16[16,192]{1,0:T(8,128)(2,1)S(1)} %convert.108), channel_id=1, source_target_pairs={{0,48},{4,52},{8,56},{12,60},{16,64},{20,68},{24,72},{28,76},{32,8... | collective-permute-start | bytes 18440
  309.6 304.7 %collective-permute-start.26 = (bf16[16,192]{1,0:T(8,128)(2,1)S(1)}, bf16[16,192]{1,0:T(8,128)(2,1)S(1)}, u32[]{:S(2)}, u32[]{:S(2)}) collective-permute-start(bf16[16,192]{1,0:T(8,128)(2,1)S(1)} %convert.108), channel_id=1, source_target_pairs={{0,44},{4,48},{8,52},{12,56},{16,60},{20,64},{24,68},{28,72},{32,7... | collective-permute-start | bytes 18440
  311.2 315.2 %collective-permute-start.25 = (bf16[16,192]{1,0:T(8,128)(2,1)S(1)}, bf16[16,192]{1,0:T(8,128)(2,1)S(1)}, u32[]{:S(2)}, u32[]{:S(2)}) collective-permute-start(bf16[16,192]{1,0:T(8,128)(2,1)S(1)} %convert.108), channel_id=1, source_target_pairs={{0,40},{4,44},{8,48},{12,52},{16,56},{20,60},{24,64},{28,68},{32,7... | collective-permute-start | bytes 18440
  610.4 17.4 %collective-permute-start.24 = (bf16[16,192]{1,0:T(8,128)(2,1)S(1)}, bf16[16,192]{1,0:T(8,128)(2,1)S(1)}, u32[]{:S(2)}, u32[]{:S(2)}) collective-permute-start(bf16[16,192]{1,0:T(8,128)(2,1)S(1)} %convert.108), channel_id=1, source_target_pairs={{0,36},{4,40},{8,44},{12,48},{16,52},{20,56},{24,60},{28,64},{32,6... | collective-permute-start | bytes 18440
  611.7 19.2 %collective-permute-start.23 = (bf16[16,192]{1,0:T(8,128)(2,1)S(1)}, bf16[16,192]{1,0:T(8,128)(2,1)S(1)}, u32[]{:S(2)}, u32[]{:S(2)}) collective-permute-start(bf16[16,192]{1,0:T(8,128)(2,1)S(1)} %convert.108), channel_id=1, source_target_pairs={{0,32},{4,36},{8,40},{12,44},{16,48},{20,52},{24,56},{28,60},{32,6... | collective-permute-start | bytes 18440
  613.0 22.8 %collective-permute-start.22 = (bf16[16,192]{1,0:T(8,128)(2,1)S(1)}, bf16[16,192]{1,0:T(8,128)(2,1)S(1)}, u32[]{:S(2)}, u32[]{:S(2)}) collective-permute-start(bf16[16,192]{1,0:T(8,128)(2,1)S(1)} %convert.108), channel_id=1, source_target_pairs={{0,28},{4,32},{8,36},{12,40},{16,44},{20,48},{24,52},{28,56},{32,6... | collective-permute-start | bytes 18440
  614.3 25.3 %collective-permute-start.21 = (bf16[16,192]{1,0:T(8,128)(2,1)S(1)}, bf16[16,192]{1,0:T(8,128)(2,1)S(1)}, u32[]{:S(2)}, u32[]{:S(2)}) collective-permute-start(bf16[16,192]{1,0:T(8,128)(2,1)S(1)} %convert.108), channel_id=1, source_target_pairs={{0,24},{4,28},{8,32},{12,36},{16,40},{20,44},{24,48},{28,52},{32,5... | collective-permute-start | bytes 18440
  626.4 16.3 %collective-permute-start.20 = (bf16[16,192]{1,0:T(8,128)(2,1)S(1)}, bf16[16,192]{1,0:T(8,128)(2,1)S(1)}, u32[]{:S(2)}, u32[]{:S(2)}) collective-permute-start(bf16[16,192]{1,0:T(8,128)(2,1)S(1)} %convert.108), channel_id=1, source_target_pairs={{0,20},{4,24},{8,28},{12,32},{16,36},{20,40},{24,44},{28,48},{32,5... | collective-permute-start | bytes 18440
  627.8 20.6 %collective-permute-start.19 = (bf16[16,192]{1,0:T(8,128)(2,1)S(1)}, bf16[16,192]{1,0:T(8,128)(2,1)S(1)}, u32[]{:S(2)}, u32[]{:S(2)}) collective-permute-start(bf16[16,192]{1,0:T(8,128)(2,1)S(1)} %convert.108), channel_id=1, source_target_pairs={{0,16},{4,20},{8,24},{12,28},{16,32},{20,36},{24,40},{28,44},{32,4... | collective-permute-start | bytes 18440
  630.9 21.9 %collective-permute-start.18 = (bf16[16,192]{1,0:T(8,128)(2,1)S(1)}, bf16[16,192]{1,0:T(8,128)(2,1)S(1)}, u32[]{:S(2)}, u32[]{:S(2)}) collective-permute-start(bf16[16,192]{1,0:T(8,128)(2,1)S(1)} %convert.108), channel_id=1, source_target_pairs={{0,12},{4,16},{8,20},{12,24},{16,28},{20,32},{24,36},{28,40},{32,4... | collective-permute-start | bytes 18440
  635.8 19.2 %collective-permute-start.17 = (bf16[16,192]{1,0:T(8,128)(2,1)S(1)}, bf16[16,192]{1,0:T(8,128)(2,1)S(1)}, u32[]{:S(2)}, u32[]{:S(2)}) collective-permute-start(bf16[16,192]{1,0:T(8,128)(2,1)S(1)} %convert.108), channel_id=1, source_target_pairs={{0,8},{4,12},{8,16},{12,20},{16,24},{20,28},{24,32},{28,36},{32,40... | collective-permute-start | bytes 18440
  639.6 17.4 %collective-permute-start.16 = (bf16[16,192]{1,0:T(8,128)(2,1)S(1)}, bf16[16,192]{1,0:T(8,128)(2,1)S(1)}, u32[]{:S(2)}, u32[]{:S(2)}) collective-permute-start(bf16[16,192]{1,0:T(8,128)(2,1)S(1)} %convert.108), channel_id=1, source_target_pairs={{0,4},{4,8},{8,12},{12,16},{16,20},{20,24},{24,28},{28,32},{32,36}... | collective-permute-start | bytes 18440
  642.7 17.2 %collective-permute-start.47 = (bf16[768,6]{0,1:T(8,128)(2,1)S(1)}, bf16[768,6]{0,1:T(8,128)(2,1)S(1)}, u32[]{:S(2)}, u32[]{:S(2)}) collective-permute-start(bf16[768,6]{0,1:T(8,128)(2,1)S(1)} %slice.2), channel_id=1, source_target_pairs={{0,64},{4,68},{8,72},{12,76},{16,80},{20,84},{24,88},{28,92},{32,9... | collective-permute-start | bytes 27656
  648.4 18.7 %collective-permute-start.46 = (bf16[768,8]{0,1:T(8,128)(2,1)S(1)}, bf16[768,8]{0,1:T(8,128)(2,1)S(1)}, u32[]{:S(2)}, u32[]{:S(2)}) collective-permute-start(bf16[768,8]{0,1:T(8,128)(2,1)S(1)} %convert.107), channel_id=1, source_target_pairs={{0,60},{4,64},{8,68},{12,72},{16,76},{20,80},{24,84},{28,88},{32,9... | collective-permute-start | bytes 36872
  652.8 15.6 %collective-permute-start.45 = (bf16[768,8]{0,1:T(8,128)(2,1)S(1)}, bf16[768,8]{0,1:T(8,128)(2,1)S(1)}, u32[]{:S(2)}, u32[]{:S(2)}) collective-permute-start(bf16[768,8]{0,1:T(8,128)(2,1)S(1)} %convert.107), channel_id=1, source_target_pairs={{0,56},{4,60},{8,64},{12,68},{16,72},{20,76},{24,80},{28,84},{32,8... | collective-permute-start | bytes 36872
  655.1 16.8 %collective-permute-start.44 = (bf16[768,8]{0,1:T(8,128)(2,1)S(1)}, bf16[768,8]{0,1:T(8,128)(2,1)S(1)}, u32[]{:S(2)}, u32[]{:S(2)}) collective-permute-start(bf16[768,8]{0,1:T(8,128)(2,1)S(1)} %convert.107), channel_id=1, source_target_pairs={{0,52},{4,56},{8,60},{12,64},{16,68},{20,72},{24,76},{28,80},{32,8... | collective-permute-start | bytes 36872
  657.0 16.2 %collective-permute-start.43 = (bf16[768,8]{0,1:T(8,128)(2,1)S(1)}, bf16[768,8]{0,1:T(8,128)(2,1)S(1)}, u32[]{:S(2)}, u32[]{:S(2)}) collective-permute-start(bf16[768,8]{0,1:T(8,128)(2,1)S(1)} %convert.107), channel_id=1, source_target_pairs={{0,48},{4,52},{8,56},{12,60},{16,64},{20,68},{24,72},{28,76},{32,8... | collective-permute-start | bytes 36872
  659.8 16.5 %collective-permute-start.42 = (bf16[768,8]{0,1:T(8,128)(2,1)S(1)}, bf16[768,8]{0,1:T(8,128)(2,1)S(1)}, u32[]{:S(2)}, u32[]{:S(2)}) collective-permute-start(bf16[768,8]{0,1:T(8,128)(2,1)S(1)} %convert.107), channel_id=1, source_target_pairs={{0,44},{4,48},{8,52},{12,56},{16,60},{20,64},{24,68},{28,72},{32,7... | collective-permute-start | bytes 36872
  667.1 13.8 %collective-permute-start.41 = (bf16[768,8]{0,1:T(8,128)(2,1)S(1)}, bf16[768,8]{0,1:T(8,128)(2,1)S(1)}, u32[]{:S(2)}, u32[]{:S(2)}) collective-permute-start(bf16[768,8]{0,1:T(8,128)(2,1)S(1)} %convert.107), channel_id=1, source_target_pairs={{0,40},{4,44},{8,48},{12,52},{16,56},{20,60},{24,64},{28,68},{32,7... | collective-permute-start | bytes 36872
  668.4 15.6 %collective-permute-start.40 = (bf16[768,8]{0,1:T(8,128)(2,1)S(1)}, bf16[768,8]{0,1:T(8,128)(2,1)S(1)}, u32[]{:S(2)}, u32[]{:S(2)}) collective-permute-start(bf16[768,8]{0,1:T(8,128)(2,1)S(1)} %convert.107), channel_id=1, source_target_pairs={{0,36},{4,40},{8,44},{12,48},{16,52},{20,56},{24,60},{28,64},{32,6... | collective-permute-start | bytes 36872
  671.9 14.6 %collective-permute-start.39 = (bf16[768,8]{0,1:T(8,128)(2,1)S(1)}, bf16[768,8]{0,1:T(8,128)(2,1)S(1)}, u32[]{:S(2)}, u32[]{:S(2)}) collective-permute-start(bf16[768,8]{0,1:T(8,128)(2,1)S(1)} %convert.107), channel_id=1, source_target_pairs={{0,32},{4,36},{8,40},{12,44},{16,48},{20,52},{24,56},{28,60},{32,6... | collective-permute-start | bytes 36872
  673.2 16.4 %collective-permute-start.38 = (bf16[768,8]{0,1:T(8,128)(2,1)S(1)}, bf16[768,8]{0,1:T(8,128)(2,1)S(1)}, u32[]{:S(2)}, u32[]{:S(2)}) collective-permute-start(bf16[768,8]{0,1:T(8,128)(2,1)S(1)} %convert.107), channel_id=1, source_target_pairs={{0,28},{4,32},{8,36},{12,40},{16,44},{20,48},{24,52},{28,56},{32,6... | collective-permute-start | bytes 36872
  676.3 16.1 %collective-permute-start.37 = (bf16[768,8]{0,1:T(8,128)(2,1)S(1)}, bf16[768,8]{0,1:T(8,128)(2,1)S(1)}, u32[]{:S(2)}, u32[]{:S(2)}) collective-permute-start(bf16[768,8]{0,1:T(8,128)(2,1)S(1)} %convert.107), channel_id=1, source_target_pairs={{0,24},{4,28},{8,32},{12,36},{16,40},{20,44},{24,48},{28,52},{32,5... | collective-permute-start | bytes 36872
  680.9 14.5 %collective-permute-start.36 = (bf16[768,8]{0,1:T(8,128)(2,1)S(1)}, bf16[768,8]{0,1:T(8,128)(2,1)S(1)}, u32[]{:S(2)}, u32[]{:S(2)}) collective-permute-start(bf16[768,8]{0,1:T(8,128)(2,1)S(1)} %convert.107), channel_id=1, source_target_pairs={{0,20},{4,24},{8,28},{12,32},{16,36},{20,40},{24,44},{28,48},{32,5... | collective-permute-start | bytes 36872
  684.0 11.4 %collective-permute-start.35 = (bf16[768,8]{0,1:T(8,128)(2,1)S(1)}, bf16[768,8]{0,1:T(8,128)(2,1)S(1)}, u32[]{:S(2)}, u32[]{:S(2)}) collective-permute-start(bf16[768,8]{0,1:T(8,128)(2,1)S(1)} %convert.107), channel_id=1, source_target_pairs={{0,16},{4,20},{8,24},{12,28},{16,32},{20,36},{24,40},{28,44},{32,4... | collective-permute-start | bytes 36872
  686.5 8.9 collective-permute-start.34
  689.6 5.7 collective-permute-start.33
  692.4 6.8 collective-permute-start.32
  (35 other events, 843.4 us)
